TPU v7x, 256 devices: a whole 4x4x8 slice. The times are simulated.
256 devices in a mesh: dp: 32 (over z, y), fsdp: 8 (over x, core).
Axes of the slice: x: 4, y: 4, z: 8, core: 2. Of those that a mesh axis runs over, the one named last changes fastest.
Arguments:
- frames: bfloat16 [8, 768, 32, 1536], P('fsdp', 'dp'), may hold values from -6 to 6
- ln_gain: float32 [1536], replicated, may hold values from 0.5 to 1.5
- w_in: bfloat16 [1536, 3072], P(('dp', 'fsdp')), may hold values from -0.15625 to 0.15625
- depth_kernel: float32 [31, 1536], replicated, may hold values from -1 to 1
- bn_scale: float32 [1536], replicated, may hold values from 0.5 to 1.5
- bn_shift: float32 [1536], replicated, may hold values from -3 to 3
- w_out: bfloat16 [1536, 1536], P(('dp', 'fsdp')), may hold values from -0.15625 to 0.15625
- lengths: int32 [8, 32, 24], P('fsdp'), may hold values from 0 to 32, as said below
- destinations: int32 [8, 32, 24], P('fsdp'), may hold values from 0 to 31, as said below
- offsets: int32 [8, 32, 24], P('fsdp'), may hold values from 0 to 224, as said below
Outputs:
- encoded: bfloat16 [8, 256, 32, 1536], P('fsdp', 'dp')
Inputs may be any that keep to these rules, and one draw needn't show every extreme that they name: lengths: live slots come first in a loader and hold half of 32 to 32 frames; 0 marks an empty slot. In each group the busiest loader has all 24 slots live, the group has 256 live utterances, and one of them has 32 frames. destinations: within a group a loader sends at most one live utterance to a device, and every device receives exactly 8 live utterances. Empty slots hold 0. offsets: multiples of 32; the 8 live utterances received by one device have distinct offsets. Empty slots hold 0.
All inputs are finite; a program needn't handle non-finite values.
Results may differ from a plain program's by a relative error of at most 0.003.
Values may be sent and summed in bfloat16 or wider, within the bound.
A program may use at most 128 MiB of HBM per device.

v0:
```python
import jax
import jax.numpy as jnp
from jax import lax
from jax.sharding import PartitionSpec as P


def conv_module(blocks, utt_lengths, ln_gain, depth_kernel, bn_scale, bn_shift, full_in, full_out):
    block_count, frames_len, feature_width = blocks.shape
    wide_rows = blocks.reshape(block_count * frames_len, feature_width).astype(jnp.float32)
    row_mean = jnp.mean(wide_rows, axis=1, keepdims=True)
    centred = wide_rows - row_mean
    row_var = jnp.mean(centred * centred, axis=1, keepdims=True)
    normed = (centred * lax.rsqrt(row_var + 1e-05) * ln_gain).astype(jnp.bfloat16)
    glu_in = jnp.dot(normed, full_in, preferred_element_type=jnp.float32)
    gated_units = glu_in[:, :feature_width] * jax.nn.sigmoid(glu_in[:, feature_width:])
    gated_units = gated_units.reshape(block_count, frames_len, feature_width)
    valid_mask = jnp.arange(frames_len, dtype=jnp.int32)[None, :] < utt_lengths[:, None]
    gated_units = jnp.where(valid_mask[:, :, None], gated_units, jnp.zeros((), gated_units.dtype))
    side_reach = (depth_kernel.shape[0] - 1) // 2
    padded = jnp.pad(gated_units, ((0, 0), (side_reach, side_reach), (0, 0)))
    convolved = padded[:, 0:frames_len, :] * depth_kernel[0]
    for kernel_tap in range(1, depth_kernel.shape[0]):
        convolved = (
            convolved
            + padded[:, kernel_tap : kernel_tap + frames_len, :] * depth_kernel[kernel_tap]
        )
    shifted = convolved * bn_scale + bn_shift
    activated = (shifted * jax.nn.sigmoid(shifted)).astype(jnp.bfloat16)
    activated = activated.reshape(block_count * frames_len, feature_width)
    mixed_out = wide_rows + jnp.dot(activated, full_out, preferred_element_type=jnp.float32)
    mixed_out = mixed_out.reshape(block_count, frames_len, feature_width)
    mixed_out = jnp.where(valid_mask[:, :, None], mixed_out, jnp.zeros((), mixed_out.dtype))
    return mixed_out.astype(jnp.bfloat16)


def shards(
    frames, ln_gain, w_in, depth_kernel, bn_scale, bn_shift, w_out, lengths, destinations, offsets
):
    dp_count = lax.axis_size("dp")
    dp_index = lax.axis_index("dp")
    tab_len = lengths[0]
    tab_dest = destinations[0]
    tab_off = offsets[0]
    slot_count = tab_len.shape[1]
    recv_count = slot_count // 3
    frame_slots = frames.shape[2]
    own_len = lax.dynamic_index_in_dim(tab_len, dp_index, 0, keepdims=False)
    own_dest = lax.dynamic_index_in_dim(tab_dest, dp_index, 0, keepdims=False)
    slot_ids = jnp.arange(slot_count, dtype=jnp.int32)
    peer_ids = jnp.arange(dp_count, dtype=jnp.int32)
    send_table = ((own_dest[None, :] == peer_ids[:, None]) & (own_len[None, :] > 0)).astype(
        jnp.int32
    )
    send_slot = jnp.sum(send_table * slot_ids[None, :], axis=1)
    send_live = jnp.sum(send_table, axis=1) > 0
    key_table = jnp.where(tab_len > 0, tab_dest * recv_count + tab_off // frame_slots, -1)
    targets = dp_index * recv_count + jnp.arange(recv_count, dtype=jnp.int32)
    pick_table = (key_table[None, :, :] == targets[:, None, None]).astype(jnp.int32)
    recv_source = jnp.sum(pick_table * peer_ids[None, :, None], axis=(1, 2))
    full_in, full_out = (
        lax.all_gather(w_in, ("dp", "fsdp"), axis=0, tiled=True),
        lax.all_gather(w_out, ("dp", "fsdp"), axis=0, tiled=True),
    )
    local_out = conv_module(
        frames[0], own_len, ln_gain, depth_kernel, bn_scale, bn_shift, full_in, full_out
    )
    chosen = jnp.take(local_out, send_slot, axis=0)
    arrived = lax.all_to_all(
        jnp.where(send_live[:, None, None], chosen, jnp.zeros((), local_out.dtype)),
        "dp",
        split_axis=0,
        concat_axis=0,
        tiled=True,
    )
    result = jnp.take(arrived, recv_source, axis=0)
    return result[None]


def solution(mesh):
    return jax.shard_map(
        shards,
        mesh=mesh,
        in_specs=(
            P("fsdp", "dp", None, None),
            P(),
            P(("dp", "fsdp"), None),
            P(),
            P(),
            P(),
            P(("dp", "fsdp"), None),
            P("fsdp", None, None),
            P("fsdp", None, None),
            P("fsdp", None, None),
        ),
        out_specs=P("fsdp", "dp", None, None),
        check_vma=False,
    )
```

profile of v0, /device:TPU:25, one launch (start us, length us, event | category | flops | bytes accessed | tf_op | source)
XLA Modules:
  0.0 399.6 jit_solution(12368897338125634990)
XLA Ops:
  6.6 0.7 all-gather.7.cloned.1.call-update
  7.3 0.0 all-gather.5.cloned.1.call-start
  7.3 0.7 all-gather.5.cloned.1.call-update
  8.0 2.1 convert_reduce_fusion
  10.1 0.1 div.31
  10.2 2.4 fusion.67
  12.6 0.1 rsqrt.12
  12.7 0.2 dynamic-slice_reduce_fusion
  12.9 0.2 dynamic-slice_reduce_fusion.1
  13.1 0.1 convert_reduce_fusion.1
  13.2 0.2 slice_reduce_fusion.29
  13.4 0.3 slice_reduce_fusion.30
  13.7 0.1 iota_compare_fusion
  13.8 2.2 fusion.70
  16.0 114.2 %all-gather.7.cloned.1.call-done = bf16[256,6,1536]{2,1,0:T(8,128)(2,1)} async-done(((bf16[1,6,1536]{2,1,0:T(8,128)(2,1)}), bf16[256,6,1536]{2,1,0:T(8,128)(2,1)}) %all-gather.7.cloned.1.call-update) | async-done | bytes 4718608 | tf_op jit(solution)/shard_map/all_gather | solution.py:62
  130.2 8.5 %reshape.188 = bf16[1536,1536]{1,0:T(8,128)(2,1)} reshape(bf16[256,6,1536]{2,1,0:T(8,128)(2,1)} %all-gather.7.cloned.1.call-done) | data formatting | bytes 9437184
  138.6 113.5 %all-gather.5.cloned.1.call-done = bf16[256,6,3072]{2,1,0:T(8,128)(2,1)} async-done(((bf16[1,6,3072]{2,1,0:T(8,128)(2,1)}), bf16[256,6,3072]{2,1,0:T(8,128)(2,1)}) %all-gather.5.cloned.1.call-update) | async-done | bytes 9437200 | tf_op jit(solution)/shard_map/all_gather | solution.py:61
  252.1 14.2 %reshape.186 = bf16[1536,3072]{1,0:T(8,128)(2,1)} reshape(bf16[256,6,3072]{2,1,0:T(8,128)(2,1)} %all-gather.5.cloned.1.call-done) | data formatting | bytes 18874368
  266.3 10.7 %fusion.79 = f32[768,3072]{1,0:T(8,128)S(1)} fusion(bf16[768,1536]{1,0:T(8,128)(2,1)} %fusion.70, bf16[1536,3072]{1,0:T(8,128)(2,1)} %reshape.186), kind=kOutput, calls=%fused_computation.177 | convolution fusion | flops 7247757312 | bytes 21233664 | tf_op jit(solution)/shard_map/dot_general | solution.py:14
  277.0 1.2 fusion.65
  278.3 0.4 broadcast_select_fusion
  278.7 0.4 copy-done.6
  279.1 17.8 %multiply_convert_fusion = bf16[24,32,1536]{2,1,0:T(8,128)(2,1)S(1)} fusion(f32[24,32,1536]{2,1,0:T(8,128)S(1)} %broadcast_select_fusion, f32[1536]{0:T(1024)S(1)} %copy-done.6, f32[1536]{0:T(1024)S(1)} %copy-done.7, f32[1536]{0:T(1024)S(1)} %get-tuple-element.34, f32[1536]{0:T(1024)S(1)} %get-tuple-element.35, f32[1536]{0:T(1024)S(1)} %get-tuple-element.6, ...), kind=kLoop, calls=%fused_computation.109 | loop fusion | flops 80216064 | bytes 7280640 | tf_op jit(solution)/shard_map/convert_element_type | solution.py:28
  297.0 4.0 %bitcast_add_fusion = bf16[768,1536]{1,0:T(8,128)(2,1)S(1)} fusion(bf16[1,24,32,1536]{3,2,1,0:T(8,128)(2,1)S(1)} %copy-done, bf16[768,1536]{1,0:T(8,128)(2,1)S(1)} %bitcast.34, bf16[1536,1536]{1,0:T(8,128)(2,1)S(1)} %bitcast.32), kind=kOutput, calls=%fused_computation.99 | convolution fusion | flops 3627417600 | bytes 11796480 | tf_op jit(solution)/shard_map/dot_general | solution.py:30
  301.1 0.5 select_convert_fusion
  301.5 2.5 gather_fusion
  304.0 4.0 %select_select_fusion = bf16[32,32,1536]{2,1,0:T(8,128)(2,1)} fusion(bf16[32,32,1536]{2,1,0:T(8,128)(2,1)} %gather_fusion, pred[32]{0:T(512)(128)(4,1)S(1)} %get-tuple-element.38, pred[32]{0:T(512)(128)(4,1)S(1)} %get-tuple-element.39), kind=kLoop, calls=%fused_computation.110 | loop fusion | flops 3145728 | bytes 6291520 | tf_op jit(solution)/shard_map/jit(_where)/select_n | solution.py:69
  308.0 7.1 %all-to-all-start = ((bf16[32,32,1536]{2,1,0:T(8,128)(2,1)}), bf16[32,32,1536]{2,1,0:T(8,128)(2,1)}, u32[]{:S(2)}, u32[]{:S(2)}) async-start(bf16[32,32,1536]{2,1,0:T(8,128)(2,1)} %select_select_fusion), calls=%async_computation | async-start | bytes 6291456 | tf_op jit(solution)/shard_map/all_to_all | solution.py:68
  315.2 0.3 select_reduce_fusion
  315.5 73.8 %all-to-all-done = bf16[32,32,1536]{2,1,0:T(8,128)(2,1)} async-done(((bf16[32,32,1536]{2,1,0:T(8,128)(2,1)}), bf16[32,32,1536]{2,1,0:T(8,128)(2,1)}, u32[]{:S(2)}, u32[]{:S(2)}) %all-to-all-start) | async-done | bytes 3145760 | tf_op jit(solution)/shard_map/all_to_all | solution.py:68
  389.3 2.5 gather_fusion.1
  391.8 1.0 bitcast_select_fusion
  (32 shorter events, 0.2 us)
Async XLA Ops:
  6.5 7.3 %copy-start = (bf16[1,24,32,1536]{3,2,1,0:T(8,128)(2,1)S(1)}, bf16[1,24,32,1536]{3,2,1,0:T(8,128)(2,1)}, u32[]{:S(2)}) copy-start(bf16[1,24,32,1536]{3,2,1,0:T(8,128)(2,1)} %param.10) | copy-start | bytes 7077892
  6.5 6.1 %copy-start.2 = (s32[1,32,24]{1,2,0:T(8,128)S(1)}, s32[1,32,24]{1,2,0:T(8,128)}, u32[]{:S(2)}) copy-start(s32[1,32,24]{1,2,0:T(8,128)} %param.17) | copy-start | bytes 9220
  6.5 6.3 %copy-start.3 = (s32[1,32,24]{1,2,0:T(8,128)S(1)}, s32[1,32,24]{1,2,0:T(8,128)}, u32[]{:S(2)}) copy-start(s32[1,32,24]{1,2,0:T(8,128)} %param.18) | copy-start | bytes 9220
  6.5 6.7 %copy-start.1 = (f32[31,1536]{1,0:T(8,128)S(1)}, f32[31,1536]{1,0:T(8,128)}, u32[]{:S(2)}) copy-start(f32[31,1536]{1,0:T(8,128)} %param.13) | copy-start | bytes 571396
  6.5 7.3 %copy-start.5 = (f32[1536]{0:T(1024)S(1)}, f32[1536]{0:T(1024)}, u32[]{:S(2)}) copy-start(f32[1536]{0:T(1024)} %param.11) | copy-start | bytes 18436
  6.5 123.6 %all-gather.7.cloned.1.call-start = ((), (), s32[]{:S(2)}) async-start(), calls=%async_computation.2 | async-start | bytes 6316032 | tf_op jit(solution)/shard_map/all_gather | solution.py:62
  7.3 244.8 %all-gather.5.cloned.1.call-start = ((), (), s32[]{:S(2)}) async-start(), calls=%async_computation.1 | async-start | bytes 12632064 | tf_op jit(solution)/shard_map/all_gather | solution.py:61
  278.2 18.7 %slice-start = ((s8[4718592]{0:T(1024)(128)(4,1)}), s8[4194304]{0:T(1024)(128)(4,1)S(1)}, s32[]{:S(2)}) async-start(s8[4718592]{0:T(1024)(128)(4,1)} %bitcast.31), calls=%async_computation.3 | async-start | bytes 8388608
  278.3 0.8 copy-start.6
  278.3 0.9 copy-start.7
  278.3 18.7 %slice-start.1 = ((s8[4718592]{0:T(1024)(128)(4,1)}), s8[524288]{0:T(1024)(128)(4,1)S(1)}, s32[]{:S(2)}) async-start(s8[4718592]{0:T(1024)(128)(4,1)} %bitcast.31), calls=%async_computation.4 | async-start | bytes 1048576
  308.0 7.1 %copy-start.4 = (s32[1,32,24]{1,2,0:T(8,128)S(1)}, s32[1,32,24]{1,2,0:T(8,128)}, u32[]{:S(2)}) copy-start(s32[1,32,24]{1,2,0:T(8,128)} %param.19) | copy-start | bytes 9220
  308.0 81.3 %all-to-all-start = ((bf16[32,32,1536]{2,1,0:T(8,128)(2,1)}), bf16[32,32,1536]{2,1,0:T(8,128)(2,1)}, u32[]{:S(2)}, u32[]{:S(2)}) async-start(bf16[32,32,1536]{2,1,0:T(8,128)(2,1)} %select_select_fusion), calls=%async_computation | async-start | bytes 6291456 | tf_op jit(solution)/shard_map/all_to_all | solution.py:68
Sparse Core Ops, SparseCore 0:
  11.1 119.0 all-gather.6
  133.9 118.1 all-gather.4
where the time goes:
time: 400 us
  waiting for transfers between devices  303 us (76%)
  other arithmetic  32.1 us (8%)
  local copies, waits for them, and re-layouts  29.1 us (7%)
  matrix products  14.8 us (4%)
  between operations  13.6 us (3%)
  starting transfers between devices  7.2 us (2%)
    all_gather x1, waiting for transfers between devices, shards(): lax.all_gather(w_out, ('dp', 'fsdp'), axis=0, tiled=True)  114 us
    all_gather x1, waiting for transfers between devices, shards(): lax.all_gather(w_in, ('dp', 'fsdp'), axis=0, tiled=True)  113 us
    all_to_all x1, waiting for transfers between devices, shards(): lax.all_to_all(jnp.where(send_live[:, None, None], chosen, jnp.zeros((),...  73.8 us
    unnamed x22, local copies, waits for them, and re-layouts  23.1 us
    convert_element_type x1, other arithmetic, conv_module(): activated = (shifted * jax.nn.sigmoid(shifted)).astype(jnp.bfloat16)  17.8 us
    dot_general x1, matrix products, conv_module(): glu_in = jnp.dot(normed, full_in, preferred_element_type=jnp.float32)  10.7 us
  transfers between devices with their start and end apart: 3, of which 3 were waited for; matrix products, arithmetic and copies ran while one was open for 4% of the time, Pallas kernels for 0%

commit v1 on v0

--- a/solution.py
+++ b/solution.py
@@ -58,7 +58,15 @@
     pick_table = (key_table[None, :, :] == targets[:, None, None]).astype(jnp.int32)
     recv_source = jnp.sum(pick_table * peer_ids[None, :, None], axis=(1, 2))
     full_in, full_out = (
-        lax.all_gather(w_in, ("dp", "fsdp"), axis=0, tiled=True),
+        jnp.concatenate(
+            lax.all_to_all(
+                jnp.stack([w_in] * lax.axis_size(("dp", "fsdp")), axis=0),
+                axis_name=("dp", "fsdp"),
+                split_axis=0,
+                concat_axis=0,
+            ),
+            axis=0,
+        ),
         lax.all_gather(w_out, ("dp", "fsdp"), axis=0, tiled=True),
     )
     local_out = conv_module(

time: 400 us -> 464 us (1.16)
  waiting for transfers between devices: 303 us -> 345 us
  starting transfers between devices: 7.2 us -> 24.6 us
  local copies, waits for them, and re-layouts: 29.1 us -> 34.7 us
    all_to_all x0 -> x1, waiting for transfers between devices: none -> 126 us  [shards(): lax.all_to_all(jnp.stack([w_in] * lax.axis_size(('dp', 'fsdp')), axis=0),...]
    all_gather x1 -> x0, waiting for transfers between devices: 113 us -> none  [shards(): lax.all_gather(w_in, ('dp', 'fsdp'), axis=0, tiled=True)]
    all_gather x1, waiting for transfers between devices: 114 us -> 146 us  [shards(): lax.all_gather(w_out, ('dp', 'fsdp'), axis=0, tiled=True)]
    all_to_all x0 -> x1, starting transfers between devices: none -> 15.6 us  [shards(): lax.all_to_all(jnp.stack([w_in] * lax.axis_size(('dp', 'fsdp')), axis=0),...]
    unnamed x22 -> x21, local copies, waits for them, and re-layouts: 23.1 us -> 8.88 us
    reshape x0 -> x1, local copies, waits for them, and re-layouts: none -> 14.2 us  [shards(): jnp.concatenate(lax.all_to_all(jnp.stack([w_in] * lax.axis_size(('dp', 'f...]
    another operation x0 -> x1, local copies, waits for them, and re-layouts: none -> 6.86 us  [shards(): jnp.stack([w_in] * lax.axis_size(('dp', 'fsdp')), axis=0)]
  transfers between devices with their start and end apart: 3 -> 3, of which waited for: 3 -> 3; matrix products, arithmetic and copies ran while one was open for 4% -> 3% of each run, Pallas kernels for 0% -> 0%
where the time goes in v1:
time: 464 us; the launch traced here: 462 us
  waiting for transfers between devices  345 us (74%)
  local copies, waits for them, and re-layouts  34.7 us (7%)
  other arithmetic  29.9 us (6%)
  starting transfers between devices  24.6 us (5%)
  matrix products  14.8 us (3%)
  between operations  13.7 us (3%)
    all_gather x1, waiting for transfers between devices, shards(): lax.all_gather(w_out, ('dp', 'fsdp'), axis=0, tiled=True)  146 us
    all_to_all x1, waiting for transfers between devices, shards(): lax.all_to_all(jnp.stack([w_in] * lax.axis_size(('dp', 'fsdp')), axis=0),...  126 us
    all_to_all x1, waiting for transfers between devices, shards(): lax.all_to_all(jnp.where(send_live[:, None, None], chosen, jnp.zeros((),...  71.7 us
    convert_element_type x1, other arithmetic, conv_module(): activated = (shifted * jax.nn.sigmoid(shifted)).astype(jnp.bfloat16)  17.8 us
    all_to_all x1, starting transfers between devices, shards(): lax.all_to_all(jnp.stack([w_in] * lax.axis_size(('dp', 'fsdp')), axis=0),...  15.6 us
    reshape x1, local copies, waits for them, and re-layouts, shards(): jnp.concatenate(lax.all_to_all(jnp.stack([w_in] * lax.axis_size(('dp', 'f...  14.2 us
    dot_general x1, matrix products, conv_module(): glu_in = jnp.dot(normed, full_in, preferred_element_type=jnp.float32)  10.7 us
  transfers between devices with their start and end apart: 3, of which 3 were waited for; matrix products, arithmetic and copies ran while one was open for 3% of the time, Pallas kernels for 0%

profile of v1, /device:TPU:25, one launch (start us, length us, event | category | flops | bytes accessed | tf_op | source)
XLA Modules:
  0.0 462.3 jit_solution(17268735930657591792)
XLA Ops:
  6.5 6.9 %stack.2 = bf16[256,6,3072]{2,1,0:T(8,128)(2,1)} broadcast(bf16[6,3072]{1,0:T(8,128)(2,1)} %param.12), dimensions={1,2} | broadcast | bytes 9474048 | tf_op jit(solution)/shard_map/stack | solution.py:63
  13.4 15.6 %all-to-all-start = ((bf16[256,6,3072]{2,1,0:T(8,128)(2,1)}), bf16[256,6,3072]{2,1,0:T(8,128)(2,1)}, u32[]{:S(2)}, u32[]{:S(2)}) async-start(bf16[256,6,3072]{2,1,0:T(8,128)(2,1)} %stack.2), calls=%async_computation | async-start | bytes 25165824 | tf_op jit(solution)/shard_map/all_to_all | solution.py:62
  29.1 0.2 all-gather.3.cloned.1.call-start
  29.3 0.5 all-gather.3.cloned.1.call-update
  29.8 0.2 dynamic-slice_reduce_fusion
  30.0 0.2 dynamic-slice_reduce_fusion.1
  30.2 0.1 convert_reduce_fusion.1
  30.3 0.2 slice_reduce_fusion.29
  30.5 0.3 slice_reduce_fusion.30
  30.8 0.1 iota_compare_fusion
  30.9 0.4 convert_reduce_fusion
  31.3 0.8 multiply_reduce_fusion
  32.1 2.2 multiply_convert_fusion.1
  34.3 146.4 %all-gather.3.cloned.1.call-done = bf16[256,6,1536]{2,1,0:T(8,128)(2,1)} async-done(((bf16[1,6,1536]{2,1,0:T(8,128)(2,1)}), bf16[256,6,1536]{2,1,0:T(8,128)(2,1)}) %all-gather.3.cloned.1.call-update) | async-done | bytes 4718608 | tf_op jit(solution)/shard_map/all_gather | solution.py:70
  180.7 8.4 %reshape.203 = bf16[1536,1536]{1,0:T(8,128)(2,1)} reshape(bf16[256,6,1536]{2,1,0:T(8,128)(2,1)} %all-gather.3.cloned.1.call-done) | data formatting | bytes 9437184
  189.1 126.0 %all-to-all-done = bf16[256,6,3072]{2,1,0:T(8,128)(2,1)} async-done(((bf16[256,6,3072]{2,1,0:T(8,128)(2,1)}), bf16[256,6,3072]{2,1,0:T(8,128)(2,1)}, u32[]{:S(2)}, u32[]{:S(2)}) %all-to-all-start) | async-done | bytes 9437216 | tf_op jit(solution)/shard_map/all_to_all | solution.py:62
  315.1 14.2 %reshape.181 = bf16[1536,3072]{1,0:T(8,128)(2,1)} reshape(bf16[256,6,3072]{2,1,0:T(8,128)(2,1)} %all-to-all-done) | data formatting | bytes 18874368 | tf_op jit(solution)/shard_map/reshape | solution.py:61
  329.3 10.7 %fusion.74 = f32[768,3072]{1,0:T(8,128)S(1)} fusion(bf16[768,1536]{1,0:T(8,128)(2,1)} %bitcast.26, bf16[1536,3072]{1,0:T(8,128)(2,1)} %reshape.181), kind=kOutput, calls=%fused_computation.172 | convolution fusion | flops 7247757312 | bytes 21233664 | tf_op jit(solution)/shard_map/dot_general | solution.py:14
  340.0 1.2 fusion.65
  341.3 0.4 broadcast_select_fusion
  341.7 0.4 copy-done.6
  342.1 0.0 copy-done.7
  342.2 17.8 %multiply_convert_fusion = bf16[24,32,1536]{2,1,0:T(8,128)(2,1)S(1)} fusion(f32[24,32,1536]{2,1,0:T(8,128)S(1)} %broadcast_select_fusion, f32[1536]{0:T(1024)S(1)} %copy-done.6, f32[1536]{0:T(1024)S(1)} %copy-done.7, f32[1536]{0:T(1024)S(1)} %get-tuple-element.34, f32[1536]{0:T(1024)S(1)} %get-tuple-element.35, f32[1536]{0:T(1024)S(1)} %get-tuple-element.6, ...), kind=kLoop, calls=%fused_computation.101 | loop fusion | flops 80216064 | bytes 7280640 | tf_op jit(solution)/shard_map/convert_element_type | solution.py:28
  360.0 4.0 bitcast_add_fusion
  364.1 0.5 select_convert_fusion
  364.6 2.4 gather_fusion
  367.0 4.0 select_select_fusion
  370.9 8.8 %all-to-all-start.1 = ((bf16[32,32,1536]{2,1,0:T(8,128)(2,1)}), bf16[32,32,1536]{2,1,0:T(8,128)(2,1)S(1)}, u32[]{:S(2)}, u32[]{:S(2)}) async-start(bf16[32,32,1536]{2,1,0:T(8,128)(2,1)} %select_select_fusion), calls=%async_computation.1 | async-start | bytes 6291456 | tf_op jit(solution)/shard_map/all_to_all | solution.py:76
  379.8 0.3 select_reduce_fusion
  380.1 71.7 %all-to-all-done.1 = bf16[32,32,1536]{2,1,0:T(8,128)(2,1)S(1)} async-done(((bf16[32,32,1536]{2,1,0:T(8,128)(2,1)}), bf16[32,32,1536]{2,1,0:T(8,128)(2,1)S(1)}, u32[]{:S(2)}, u32[]{:S(2)}) %all-to-all-start.1) | async-done | bytes 3145760 | tf_op jit(solution)/shard_map/all_to_all | solution.py:76
  451.8 1.5 gather_fusion.1
  453.3 2.2 bitcast_select_fusion
  (30 shorter events, 0.1 us)
Async XLA Ops:
  13.4 16.4 %copy-start.2 = (s32[1,32,24]{1,2,0:T(8,128)S(1)}, s32[1,32,24]{1,2,0:T(8,128)}, u32[]{:S(2)}) copy-start(s32[1,32,24]{1,2,0:T(8,128)} %param.17) | copy-start | bytes 9220
  13.4 16.6 %copy-start.3 = (s32[1,32,24]{1,2,0:T(8,128)S(1)}, s32[1,32,24]{1,2,0:T(8,128)}, u32[]{:S(2)}) copy-start(s32[1,32,24]{1,2,0:T(8,128)} %param.18) | copy-start | bytes 9220
  13.4 16.9 %copy-start.1 = (f32[31,1536]{1,0:T(8,128)S(1)}, f32[31,1536]{1,0:T(8,128)}, u32[]{:S(2)}) copy-start(f32[31,1536]{1,0:T(8,128)} %param.13) | copy-start | bytes 571396
  13.4 17.5 %copy-start = (bf16[1,24,32,1536]{3,2,1,0:T(8,128)(2,1)S(1)}, bf16[1,24,32,1536]{3,2,1,0:T(8,128)(2,1)}, u32[]{:S(2)}) copy-start(bf16[1,24,32,1536]{3,2,1,0:T(8,128)(2,1)} %param.10) | copy-start | bytes 7077892
  13.4 301.7 %all-to-all-start = ((bf16[256,6,3072]{2,1,0:T(8,128)(2,1)}), bf16[256,6,3072]{2,1,0:T(8,128)(2,1)}, u32[]{:S(2)}, u32[]{:S(2)}) async-start(bf16[256,6,3072]{2,1,0:T(8,128)(2,1)} %stack.2), calls=%async_computation | async-start | bytes 25165824 | tf_op jit(solution)/shard_map/all_to_all | solution.py:62
  29.0 3.1 copy-start.5
  29.1 151.7 %all-gather.3.cloned.1.call-start = ((), (), s32[]{:S(2)}) async-start(), calls=%async_computation.2 | async-start | bytes 6316032 | tf_op jit(solution)/shard_map/all_gather | solution.py:70
  341.3 18.7 %slice-start = ((s8[4718592]{0:T(1024)(128)(4,1)}), s8[4194304]{0:T(1024)(128)(4,1)S(1)}, s32[]{:S(2)}) async-start(s8[4718592]{0:T(1024)(128)(4,1)} %bitcast.24), calls=%async_computation.3 | async-start | bytes 8388608
  341.3 0.8 copy-start.6
  341.3 0.9 copy-start.7
  341.3 18.7 %slice-start.1 = ((s8[4718592]{0:T(1024)(128)(4,1)}), s8[524288]{0:T(1024)(128)(4,1)S(1)}, s32[]{:S(2)}) async-start(s8[4718592]{0:T(1024)(128)(4,1)} %bitcast.24), calls=%async_computation.4 | async-start | bytes 1048576
  370.9 8.8 %copy-start.4 = (s32[1,32,24]{1,2,0:T(8,128)S(1)}, s32[1,32,24]{1,2,0:T(8,128)}, u32[]{:S(2)}) copy-start(s32[1,32,24]{1,2,0:T(8,128)} %param.19) | copy-start | bytes 9220
  370.9 80.9 %all-to-all-start.1 = ((bf16[32,32,1536]{2,1,0:T(8,128)(2,1)}), bf16[32,32,1536]{2,1,0:T(8,128)(2,1)S(1)}, u32[]{:S(2)}, u32[]{:S(2)}) async-start(bf16[32,32,1536]{2,1,0:T(8,128)(2,1)} %select_select_fusion), calls=%async_computation.1 | async-start | bytes 6291456 | tf_op jit(solution)/shard_map/all_to_all | solution.py:76
Sparse Core Ops, SparseCore 0:
  33.6 147.0 all-gather.2
